TPU v7x, 256 devices: a whole 4x4x8 slice. The times are simulated.
256 devices in a mesh: tile: 64 (over z, y_lo, x), chan: 4 (over y_hi, core).
Axes of the slice: x: 4, y: 4 (y_hi: 2, y_lo: 2; y = y_hi * 2 + y_lo), z: 8, core: 2. Of those that a mesh axis runs over, the one named last changes fastest.
Arguments:
- latent: bfloat16 [2, 16, 14400], P(None, 'chan', 'tile'), may hold values from -6 to 6
- latent_cache: bfloat16 [2, 16, 14400], P(None, 'chan', 'tile'), may hold values from -6 to 6
- weight_in: bfloat16 [3, 3, 3, 384, 16], P(None, None, None, 'chan'), may hold values from -0.3125 to 0.3125
- bias_in: float32 [384], P('chan'), may hold values from -3 to 3
- cache_a: bfloat16 [2, 384, 14400], P(None, 'chan', 'tile'), may hold values from -6 to 6
- gain_a: float32 [384], P('chan'), may hold values from 0.1 to 1.9
- weight_a: bfloat16 [3, 3, 3, 384, 384], P(None, None, None, 'chan'), may hold values from -0.0625 to 0.0625
- bias_a: float32 [384], P('chan'), may hold values from -3 to 3
- cache_b: bfloat16 [2, 384, 14400], P(None, 'chan', 'tile'), may hold values from -6 to 6
- gain_b: float32 [384], P('chan'), may hold values from 0.1 to 1.9
- weight_b: bfloat16 [3, 3, 3, 384, 384], P(None, None, None, 'chan'), may hold values from -0.0625 to 0.0625
- bias_b: float32 [384], P('chan'), may hold values from -3 to 3
- weight_up: bfloat16 [3, 3, 192, 384], P(None, None, 'chan'), may hold values from -0.109375 to 0.109375
- bias_up: float32 [192], P('chan'), may hold values from -3 to 3
Outputs:
- upsampled: bfloat16 [2, 192, 57600], P(None, 'chan', 'tile')
All inputs are finite; a program needn't handle non-finite values.
Results may differ from a plain program's by a relative error of at most 0.011.
Values may be sent and summed in bfloat16 or wider, within the bound.
A program may use at most 64 MiB of HBM per device.

v0:
```python
from functools import partial
import jax
import jax.numpy as jnp
from jax import lax
from jax.sharding import PartitionSpec as P

C = 384
W = 160
eps_norm = 1e-06


def extended(block, sides, width):
    for axis, dim in sides:
        count = lax.axis_size(axis)
        forward = [(i, i + 1) for i in range(count - 1)]
        backward = [(target, source) for source, target in forward]
        low = lax.ppermute(
            lax.slice_in_dim(block, block.shape[dim] - width, None, axis=dim), axis, forward
        )
        high = lax.ppermute(lax.slice_in_dim(block, 0, width, axis=dim), axis, backward)
        block = jnp.concatenate([low, block, high], axis=dim)
    return block


def column_mask(part, column_tap, position):
    if column_tap == 0:
        return jnp.where(position > 0, part, 0.0)
    if column_tap == 2:
        return jnp.where(position < W - 1, part, 0.0)
    return part


def causal_terms(source, weight_rows, start):
    frames = source.shape[0] - 2
    count = source.shape[2] - 2 * W - 2
    position = (start + lax.iota(jnp.int32, count)) % W
    outputs = weight_rows.shape[3]
    summed = jnp.zeros((frames, outputs, count), jnp.float32)
    for column_tap in range(3):
        part = jnp.zeros((frames, outputs, count), jnp.float32)
        for time_tap in range(3):
            for row_tap in range(3):
                begin = row_tap * W + column_tap
                window = source[time_tap : time_tap + frames, :, begin : begin + count]
                part = part + jnp.einsum(
                    "ok,fkr->for",
                    weight_rows[time_tap, row_tap, column_tap],
                    window,
                    preferred_element_type=jnp.float32,
                )
        summed = summed + column_mask(part, column_tap, position)
    return summed


def upsample_terms(source, weight_rows, start):
    frames = source.shape[0]
    count = source.shape[2] - 2 * W - 2
    position = (start + lax.iota(jnp.int32, count)) % W
    outputs = weight_rows.shape[2]
    quarters = []
    for row_half in range(2):
        for column_half in range(2):
            summed = jnp.zeros((frames, outputs, count), jnp.float32)
            for column_step in range(3):
                part = jnp.zeros((frames, outputs, count), jnp.float32)
                for row_tap in range(3):
                    row_step = (row_half + row_tap - 1) // 2
                    for column_tap in range(3):
                        if (column_half + column_tap - 1) // 2 != column_step - 1:
                            continue
                        begin = (row_step + 1) * W + column_step
                        window = source[:, :, begin : begin + count]
                        part = part + jnp.einsum(
                            "ok,fkr->for",
                            weight_rows[row_tap, column_tap],
                            window,
                            preferred_element_type=jnp.float32,
                        )
                summed = summed + column_mask(part, column_step, position)
            quarters.append(summed)
    stacked = jnp.stack(quarters, -1)
    return stacked.reshape(frames, outputs, 4 * count)


def convolve(source, weight, kernel_fn):
    complete = lax.all_gather(source, "chan", axis=1, tiled=True)
    rimmed = extended(complete, (("tile", 2),), W + 1)
    return kernel_fn(rimmed, weight)


def activate(features, gain_vector):
    values = features.astype(jnp.float32)
    squares = jnp.sum(values * values, axis=1)
    total_sq = lax.psum(squares, "chan")
    inverse_rms = lax.rsqrt(total_sq / C + eps_norm)
    return jax.nn.silu(values * inverse_rms[:, None, :] * gain_vector[None, :, None]).astype(
        jnp.bfloat16
    )


def shards(
    latent,
    latent_cache,
    weight_in,
    bias_in,
    cache_a,
    gain_a,
    weight_a,
    bias_a,
    cache_b,
    gain_b,
    weight_b,
    bias_b,
    weight_up,
    bias_up,
):
    span = latent.shape[2]
    start = lax.axis_index("tile") * span
    causal_fn = partial(causal_terms, start=start)
    upsample_fn = partial(upsample_terms, start=start)
    stem_sum = convolve(jnp.concatenate([latent_cache, latent], 0), weight_in, causal_fn)
    stem_out = (stem_sum + bias_in[None, :, None]).astype(jnp.bfloat16)
    active_a = activate(stem_out, gain_a)
    inner_sum = convolve(jnp.concatenate([cache_a, active_a], 0), weight_a, causal_fn)
    inner_out = (inner_sum + bias_a[None, :, None]).astype(jnp.bfloat16)
    active_b = activate(inner_out, gain_b)
    branch_sum = convolve(jnp.concatenate([cache_b, active_b], 0), weight_b, causal_fn)
    residual_out = (stem_out.astype(jnp.float32) + branch_sum + bias_b[None, :, None]).astype(
        jnp.bfloat16
    )
    upsample_sum = convolve(residual_out, weight_up, upsample_fn)
    return (upsample_sum + bias_up[None, :, None]).astype(jnp.bfloat16)


def solution(mesh):
    placed = (
        P(None, "chan", "tile"),
        P(None, "chan", "tile"),
        P(None, None, None, "chan", None),
        P("chan"),
        P(None, "chan", "tile"),
        P("chan"),
        P(None, None, None, "chan", None),
        P("chan"),
        P(None, "chan", "tile"),
        P("chan"),
        P(None, None, None, "chan", None),
        P("chan"),
        P(None, None, "chan", None),
        P("chan"),
    )
    return jax.shard_map(
        shards, mesh=mesh, in_specs=placed, out_specs=P(None, "chan", "tile"), check_vma=False
    )
```

profile of v0, /device:TPU:128, one launch (start us, length us, event | category | flops | bytes accessed | tf_op | source)
XLA Modules:
  0.0 182.4 jit_solution(865237823081435494)
XLA Ops:
  1.4 6.7 %all_gather.12 = bf16[4,16,225]{2,0,1:T(4,128)(2,1)S(1)} all-gather(bf16[4,4,225]{2,0,1:T(4,128)(2,1)S(1)} %pad_maximum_fusion.19), channel_id=1, replica_groups=mesh['tile'=64,'chan'=4] {'chan'}, dimensions={1}, use_global_device_ids=true | all-gather | bytes 36000 | tf_op jit(solution)/shard_map/all_gather | solution.py:86
  8.2 5.2 %collective-permute-start.1 = (bf16[4,16,161]{2,1,0:T(8,128)(2,1)S(1)}, bf16[4,16,161]{2,1,0:T(8,128)(2,1)S(1)}, u32[]{:S(2)}, u32[]{:S(2)}) collective-permute-start(bf16[4,16,161]{2,1,0:T(8,128)(2,1)S(1)} %get-tuple-element.18), channel_id=1, source_target_pairs={{4,0},{8,4},{12,8},{16,12},{20,16},{24,20},{28,24},{32,28},{36,32}... | collective-permute-start | bytes 61832 | tf_op jit(solution)/shard_map/ppermute | solution.py:20
  13.4 1.9 %collective-permute-start = (bf16[4,16,161]{2,1,0:T(8,128)(2,1)S(1)}, bf16[4,16,161]{2,1,0:T(8,128)(2,1)S(1)}, u32[]{:S(2)}, u32[]{:S(2)}) collective-permute-start(bf16[4,16,161]{2,1,0:T(8,128)(2,1)S(1)} %get-tuple-element.17), channel_id=1, source_target_pairs={{0,4},{4,8},{8,12},{12,16},{16,20},{20,24},{24,28},{28,32},{32,36}... | collective-permute-start | bytes 61832 | tf_op jit(solution)/shard_map/ppermute | solution.py:17
  28.5 8.6 %psum.14 = f32[2,225]{1,0:T(2,128)S(1)} all-reduce(f32[2,225]{1,0:T(2,128)S(1)} %get-tuple-element.19), channel_id=1, replica_groups=mesh['tile'=64,'chan'=4] {'chan'}, use_global_device_ids=true, to_apply=%region_1.2 | all-reduce | flops 450 | bytes 3600 | tf_op jit(solution)/shard_map/psum | solution.py:94
  37.3 8.9 %all_gather.13 = bf16[4,384,225]{2,1,0:T(8,128)(2,1)S(1)} all-gather(bf16[4,96,225]{2,1,0:T(8,128)(2,1)S(1)} %pad_maximum_fusion.13), channel_id=1, replica_groups=mesh['tile'=64,'chan'=4] {'chan'}, dimensions={1}, use_global_device_ids=true | all-gather | bytes 864000 | tf_op jit(solution)/shard_map/all_gather | solution.py:86
  47.4 6.6 %collective-permute-start.3 = (bf16[4,384,161]{1,0,2:T(4,128)(2,1)S(1)}, bf16[4,384,161]{1,0,2:T(4,128)(2,1)}, u32[]{:S(2)}, u32[]{:S(2)}) collective-permute-start(bf16[4,384,161]{1,0,2:T(4,128)(2,1)S(1)} %copy.259), channel_id=1, source_target_pairs={{4,0},{8,4},{12,8},{16,12},{20,16},{24,20},{28,24},{32,28},{36,32}... | collective-permute-start | bytes 1483784 | tf_op jit(solution)/shard_map/ppermute | solution.py:20
  54.9 1.9 %collective-permute-start.2 = (bf16[4,384,161]{1,0,2:T(4,128)(2,1)S(1)}, bf16[4,384,161]{1,0,2:T(4,128)(2,1)}, u32[]{:S(2)}, u32[]{:S(2)}) collective-permute-start(bf16[4,384,161]{1,0,2:T(4,128)(2,1)S(1)} %copy.255), channel_id=1, source_target_pairs={{0,4},{4,8},{8,12},{12,16},{16,20},{20,24},{24,28},{28,32},{32,36}... | collective-permute-start | bytes 1483784 | tf_op jit(solution)/shard_map/ppermute | solution.py:17
  57.9 1.8 fusion.301
  59.7 1.8 fusion.305
  61.5 3.6 %collective-permute-done.3 = bf16[4,384,161]{1,0,2:T(4,128)(2,1)} collective-permute-done((bf16[4,384,161]{1,0,2:T(4,128)(2,1)S(1)}, bf16[4,384,161]{1,0,2:T(4,128)(2,1)}, u32[]{:S(2)}, u32[]{:S(2)}) %collective-permute-start.3) | collective-permute-done | bytes 494624 | tf_op jit(solution)/shard_map/ppermute | solution.py:20
  71.7 2.6 %collective-permute-done.2 = bf16[4,384,161]{1,0,2:T(4,128)(2,1)} collective-permute-done((bf16[4,384,161]{1,0,2:T(4,128)(2,1)S(1)}, bf16[4,384,161]{1,0,2:T(4,128)(2,1)}, u32[]{:S(2)}, u32[]{:S(2)}) %collective-permute-start.2) | collective-permute-done | bytes 494624 | tf_op jit(solution)/shard_map/ppermute | solution.py:17
  86.1 8.7 %psum.15 = f32[2,225]{1,0:T(2,128)S(1)} all-reduce(f32[2,225]{1,0:T(2,128)S(1)} %get-tuple-element.21), channel_id=1, replica_groups=mesh['tile'=64,'chan'=4] {'chan'}, use_global_device_ids=true, to_apply=%region_3.4 | all-reduce | flops 450 | bytes 3600 | tf_op jit(solution)/shard_map/psum | solution.py:94
  95.0 8.7 %all_gather.14 = bf16[4,384,225]{2,1,0:T(8,128)(2,1)S(1)} all-gather(bf16[4,96,225]{2,1,0:T(8,128)(2,1)S(1)} %pad_maximum_fusion.14), channel_id=1, replica_groups=mesh['tile'=64,'chan'=4] {'chan'}, dimensions={1}, use_global_device_ids=true | all-gather | bytes 864000 | tf_op jit(solution)/shard_map/all_gather | solution.py:86
  104.9 5.8 %collective-permute-start.5 = (bf16[4,384,161]{1,0,2:T(4,128)(2,1)S(1)}, bf16[4,384,161]{1,0,2:T(4,128)(2,1)}, u32[]{:S(2)}, u32[]{:S(2)}) collective-permute-start(bf16[4,384,161]{1,0,2:T(4,128)(2,1)S(1)} %copy.290), channel_id=1, source_target_pairs={{4,0},{8,4},{12,8},{16,12},{20,16},{24,20},{28,24},{32,28},{36,32}... | collective-permute-start | bytes 1483784 | tf_op jit(solution)/shard_map/ppermute | solution.py:20
  111.6 1.9 %collective-permute-start.4 = (bf16[4,384,161]{1,0,2:T(4,128)(2,1)S(1)}, bf16[4,384,161]{1,0,2:T(4,128)(2,1)}, u32[]{:S(2)}, u32[]{:S(2)}) collective-permute-start(bf16[4,384,161]{1,0,2:T(4,128)(2,1)S(1)} %copy.286), channel_id=1, source_target_pairs={{0,4},{4,8},{8,12},{12,16},{16,20},{20,24},{24,28},{28,32},{32,36}... | collective-permute-start | bytes 1483784 | tf_op jit(solution)/shard_map/ppermute | solution.py:17
  114.7 1.8 fusion.271
  116.4 1.8 fusion.275
  118.2 3.6 %collective-permute-done.5 = bf16[4,384,161]{1,0,2:T(4,128)(2,1)} collective-permute-done((bf16[4,384,161]{1,0,2:T(4,128)(2,1)S(1)}, bf16[4,384,161]{1,0,2:T(4,128)(2,1)}, u32[]{:S(2)}, u32[]{:S(2)}) %collective-permute-start.5) | collective-permute-done | bytes 494624 | tf_op jit(solution)/shard_map/ppermute | solution.py:20
  128.5 2.6 %collective-permute-done.4 = bf16[4,384,161]{1,0,2:T(4,128)(2,1)} collective-permute-done((bf16[4,384,161]{1,0,2:T(4,128)(2,1)S(1)}, bf16[4,384,161]{1,0,2:T(4,128)(2,1)}, u32[]{:S(2)}, u32[]{:S(2)}) %collective-permute-start.4) | collective-permute-done | bytes 494624 | tf_op jit(solution)/shard_map/ppermute | solution.py:17
  142.9 7.7 %all_gather.15 = bf16[2,384,225]{2,1,0:T(8,128)(2,1)S(1)} all-gather(bf16[2,96,225]{2,1,0:T(8,128)(2,1)S(1)} %fusion.76), channel_id=1, replica_groups=mesh['tile'=64,'chan'=4] {'chan'}, dimensions={1}, use_global_device_ids=true | all-gather | bytes 432000 | tf_op jit(solution)/shard_map/all_gather | solution.py:86
  151.5 6.1 %collective-permute-start.7 = (bf16[2,384,161]{2,1,0:T(8,128)(2,1)S(1)}, bf16[2,384,161]{2,1,0:T(8,128)(2,1)S(1)}, u32[]{:S(2)}, u32[]{:S(2)}) collective-permute-start(bf16[2,384,161]{2,1,0:T(8,128)(2,1)S(1)} %get-tuple-element.16), channel_id=1, source_target_pairs={{4,0},{8,4},{12,8},{16,12},{20,16},{24,20},{28,24},{32,28},{36,32}... | collective-permute-start | bytes 741896 | tf_op jit(solution)/shard_map/ppermute | solution.py:20
  157.6 2.1 %collective-permute-start.6 = (bf16[2,384,161]{2,1,0:T(8,128)(2,1)S(1)}, bf16[2,384,161]{2,1,0:T(8,128)(2,1)S(1)}, u32[]{:S(2)}, u32[]{:S(2)}) collective-permute-start(bf16[2,384,161]{2,1,0:T(8,128)(2,1)S(1)} %get-tuple-element.15), channel_id=1, source_target_pairs={{0,4},{4,8},{8,12},{12,16},{16,20},{20,24},{24,28},{28,32},{32,36}... | collective-permute-start | bytes 741896 | tf_op jit(solution)/shard_map/ppermute | solution.py:17
  160.1 6.3 %collective-permute-done.7 = bf16[2,384,161]{2,1,0:T(8,128)(2,1)S(1)} collective-permute-done((bf16[2,384,161]{2,1,0:T(8,128)(2,1)S(1)}, bf16[2,384,161]{2,1,0:T(8,128)(2,1)S(1)}, u32[]{:S(2)}, u32[]{:S(2)}) %collective-permute-start.7) | collective-permute-done | bytes 247328 | tf_op jit(solution)/shard_map/ppermute | solution.py:20
  166.5 8.3 %collective-permute-done.6 = bf16[2,384,161]{2,1,0:T(8,128)(2,1)S(1)} collective-permute-done((bf16[2,384,161]{2,1,0:T(8,128)(2,1)S(1)}, bf16[2,384,161]{2,1,0:T(8,128)(2,1)S(1)}, u32[]{:S(2)}, u32[]{:S(2)}) %collective-permute-start.6) | collective-permute-done | bytes 247328 | tf_op jit(solution)/shard_map/ppermute | solution.py:17
  (164 shorter events, 66.3 us)
Async XLA Ops:
  0.0 23.5 %copy-start.7 = (bf16[3,3,3,96,16]{3,4,2,1,0:T(8,128)(2,1)S(1)}, bf16[3,3,3,96,16]{3,4,2,1,0:T(8,128)(2,1)}, u32[]{:S(2)}) copy-start(bf16[3,3,3,96,16]{3,4,2,1,0:T(8,128)(2,1)} %param.16) | copy-start | bytes 248836
  8.2 9.9 %collective-permute-start.1 = (bf16[4,16,161]{2,1,0:T(8,128)(2,1)S(1)}, bf16[4,16,161]{2,1,0:T(8,128)(2,1)S(1)}, u32[]{:S(2)}, u32[]{:S(2)}) collective-permute-start(bf16[4,16,161]{2,1,0:T(8,128)(2,1)S(1)} %get-tuple-element.18), channel_id=1, source_target_pairs={{4,0},{8,4},{12,8},{16,12},{20,16},{24,20},{28,24},{32,28},{36,32}... | collective-permute-start | bytes 61832 | tf_op jit(solution)/shard_map/ppermute | solution.py:20
  13.4 10.0 %collective-permute-start = (bf16[4,16,161]{2,1,0:T(8,128)(2,1)S(1)}, bf16[4,16,161]{2,1,0:T(8,128)(2,1)S(1)}, u32[]{:S(2)}, u32[]{:S(2)}) collective-permute-start(bf16[4,16,161]{2,1,0:T(8,128)(2,1)S(1)} %get-tuple-element.17), channel_id=1, source_target_pairs={{0,4},{4,8},{8,12},{12,16},{16,20},{20,24},{24,28},{28,32},{32,36}... | collective-permute-start | bytes 61832 | tf_op jit(solution)/shard_map/ppermute | solution.py:17
  27.6 0.7 copy-start.10
  27.6 9.5 %copy-start.11 = (f32[96]{0:T(128)S(1)}, f32[96]{0:T(128)}, u32[]{:S(2)}) copy-start(f32[96]{0:T(128)} %param.19) | copy-start | bytes 1156
  27.6 9.6 %copy-start.8 = (bf16[2,96,225]{2,1,0:T(8,128)(2,1)S(1)}, bf16[2,96,225]{2,1,0:T(8,128)(2,1)}, u32[]{:S(2)}) copy-start(bf16[2,96,225]{2,1,0:T(8,128)(2,1)} %param.18) | copy-start | bytes 259204
  47.4 17.6 %collective-permute-start.3 = (bf16[4,384,161]{1,0,2:T(4,128)(2,1)S(1)}, bf16[4,384,161]{1,0,2:T(4,128)(2,1)}, u32[]{:S(2)}, u32[]{:S(2)}) collective-permute-start(bf16[4,384,161]{1,0,2:T(4,128)(2,1)S(1)} %copy.259), channel_id=1, source_target_pairs={{4,0},{8,4},{12,8},{16,12},{20,16},{24,20},{28,24},{32,28},{36,32}... | collective-permute-start | bytes 1483784 | tf_op jit(solution)/shard_map/ppermute | solution.py:20
  54.9 19.5 %collective-permute-start.2 = (bf16[4,384,161]{1,0,2:T(4,128)(2,1)S(1)}, bf16[4,384,161]{1,0,2:T(4,128)(2,1)}, u32[]{:S(2)}, u32[]{:S(2)}) collective-permute-start(bf16[4,384,161]{1,0,2:T(4,128)(2,1)S(1)} %copy.255), channel_id=1, source_target_pairs={{0,4},{4,8},{8,12},{12,16},{16,20},{20,24},{24,28},{28,32},{32,36}... | collective-permute-start | bytes 1483784 | tf_op jit(solution)/shard_map/ppermute | solution.py:17
  75.9 2.7 %copy-start.1 = (bf16[3,3,3,96,384]{4,3,2,1,0:T(8,128)(2,1)S(1)}, bf16[3,3,3,96,384]{4,3,2,1,0:T(8,128)(2,1)}, u32[]{:S(2)}) copy-start(bf16[3,3,3,96,384]{4,3,2,1,0:T(8,128)(2,1)} %param.20) | copy-start | bytes 5971972
  82.7 0.9 copy-start.3
  82.7 1.0 copy-start.4
  85.0 0.7 copy-start.12
  85.7 9.1 %copy-start.13 = (f32[96]{0:T(128)S(1)}, f32[96]{0:T(128)}, u32[]{:S(2)}) copy-start(f32[96]{0:T(128)} %param.23) | copy-start | bytes 1156
  85.7 9.3 %copy-start.9 = (bf16[2,96,225]{2,1,0:T(8,128)(2,1)S(1)}, bf16[2,96,225]{2,1,0:T(8,128)(2,1)}, u32[]{:S(2)}) copy-start(bf16[2,96,225]{2,1,0:T(8,128)(2,1)} %param.22) | copy-start | bytes 259204
  104.9 16.9 %collective-permute-start.5 = (bf16[4,384,161]{1,0,2:T(4,128)(2,1)S(1)}, bf16[4,384,161]{1,0,2:T(4,128)(2,1)}, u32[]{:S(2)}, u32[]{:S(2)}) collective-permute-start(bf16[4,384,161]{1,0,2:T(4,128)(2,1)S(1)} %copy.290), channel_id=1, source_target_pairs={{4,0},{8,4},{12,8},{16,12},{20,16},{24,20},{28,24},{32,28},{36,32}... | collective-permute-start | bytes 1483784 | tf_op jit(solution)/shard_map/ppermute | solution.py:20
  111.6 19.5 %collective-permute-start.4 = (bf16[4,384,161]{1,0,2:T(4,128)(2,1)S(1)}, bf16[4,384,161]{1,0,2:T(4,128)(2,1)}, u32[]{:S(2)}, u32[]{:S(2)}) collective-permute-start(bf16[4,384,161]{1,0,2:T(4,128)(2,1)S(1)} %copy.286), channel_id=1, source_target_pairs={{0,4},{4,8},{8,12},{12,16},{16,20},{20,24},{24,28},{28,32},{32,36}... | collective-permute-start | bytes 1483784 | tf_op jit(solution)/shard_map/ppermute | solution.py:17
  132.7 2.7 %copy-start.2 = (bf16[3,3,3,96,384]{4,3,2,1,0:T(8,128)(2,1)S(1)}, bf16[3,3,3,96,384]{4,3,2,1,0:T(8,128)(2,1)}, u32[]{:S(2)}) copy-start(bf16[3,3,3,96,384]{4,3,2,1,0:T(8,128)(2,1)} %param.24) | copy-start | bytes 5971972
  139.5 0.9 copy-start.5
  139.5 1.0 copy-start.6
  141.8 0.7 copy-start.15
  142.4 8.3 %copy-start = (bf16[3,3,48,384]{3,2,1,0:T(8,128)(2,1)S(1)}, bf16[3,3,48,384]{3,2,1,0:T(8,128)(2,1)}, u32[]{:S(2)}) copy-start(bf16[3,3,48,384]{3,2,1,0:T(8,128)(2,1)} %param.26) | copy-start | bytes 995332
  151.5 15.0 %collective-permute-start.7 = (bf16[2,384,161]{2,1,0:T(8,128)(2,1)S(1)}, bf16[2,384,161]{2,1,0:T(8,128)(2,1)S(1)}, u32[]{:S(2)}, u32[]{:S(2)}) collective-permute-start(bf16[2,384,161]{2,1,0:T(8,128)(2,1)S(1)} %get-tuple-element.16), channel_id=1, source_target_pairs={{4,0},{8,4},{12,8},{16,12},{20,16},{24,20},{28,24},{32,28},{36,32}... | collective-permute-start | bytes 741896 | tf_op jit(solution)/shard_map/ppermute | solution.py:20
  157.6 17.2 %collective-permute-start.6 = (bf16[2,384,161]{2,1,0:T(8,128)(2,1)S(1)}, bf16[2,384,161]{2,1,0:T(8,128)(2,1)S(1)}, u32[]{:S(2)}, u32[]{:S(2)}) collective-permute-start(bf16[2,384,161]{2,1,0:T(8,128)(2,1)S(1)} %get-tuple-element.15), channel_id=1, source_target_pairs={{0,4},{4,8},{8,12},{12,16},{16,20},{20,24},{24,28},{28,32},{32,36}... | collective-permute-start | bytes 741896 | tf_op jit(solution)/shard_map/ppermute | solution.py:17
  180.1 1.6 copy-start.14
where the time goes:
time: 184 us; the launch traced here: 182 us
  matrix products  54.8 us (30%)
  blocking collectives  49.3 us (27%)
  starting transfers between devices  31.7 us (17%)
  waiting for transfers between devices  28.7 us (16%)
  local copies, waits for them, and re-layouts  14.8 us (8%)
  other arithmetic  2.17 us (1%)
    dot_general x81, matrix products, causal_terms(): jnp.einsum('ok,fkr->for', weight_rows[time_tap, row_tap, column_tap], win...  49.7 us
    all_gather x4, blocking collectives, convolve(): complete = lax.all_gather(source, 'chan', axis=1, tiled=True)  32 us
    ppermute x4, starting transfers between devices, extended(): lax.ppermute(lax.slice_in_dim(block, 0, width, axis=dim), axis, backward)  23.8 us
    psum x2, blocking collectives, activate(): total_sq = lax.psum(squares, 'chan')  17.2 us
    ppermute x4, waiting for transfers between devices, extended(): lax.ppermute(lax.slice_in_dim(block, block.shape[dim] - width, None, axis...  15.2 us
    ppermute x4, waiting for transfers between devices, extended(): lax.ppermute(lax.slice_in_dim(block, 0, width, axis=dim), axis, backward)  13.5 us
    ppermute x4, starting transfers between devices, extended(): lax.ppermute(lax.slice_in_dim(block, block.shape[dim] - width, None, axis...  7.9 us
    dot_general x25, matrix products, upsample_terms(): jnp.einsum('ok,fkr->for', weight_rows[row_tap, column_tap], window, prefe...  5.11 us
  transfers between devices with their start and end apart: 8, of which 7 were waited for; matrix products, arithmetic and copies ran while one was open for 17% of the time, Pallas kernels for 0%

commit v1 on v0

--- a/solution.py
+++ b/solution.py
@@ -83,7 +83,15 @@
 
 
 def convolve(source, weight, kernel_fn):
-    complete = lax.all_gather(source, "chan", axis=1, tiled=True)
+    complete = jnp.concatenate(
+        jax.lax.all_to_all(
+            jnp.stack([source for _ in range(jax.lax.axis_size("chan"))], axis=0),
+            concat_axis=0,
+            split_axis=0,
+            axis_name="chan",
+        ),
+        axis=1,
+    )
     rimmed = extended(complete, (("tile", 2),), W + 1)
     return kernel_fn(rimmed, weight)
 

time: 184 us -> 176 us (0.957)
  matrix products: 54.8 us -> 31.7 us
  waiting for transfers between devices: 28.7 us -> 45.3 us
  local copies, waits for them, and re-layouts: 14.8 us -> 6.49 us
  blocking collectives: 49.3 us -> 57.4 us
    all_to_all x0 -> x3, blocking collectives: none -> 42.7 us  [convolve(): jax.lax.all_to_all(jnp.stack([source for _ in range(jax.lax.axis_size('ch...]
    all_gather x4 -> x0, blocking collectives: 32 us -> none  [convolve(): complete = lax.all_gather(source, 'chan', axis=1, tiled=True)]
    dot_general x81, matrix products: 49.7 us -> 26 us  [causal_terms(): jnp.einsum('ok,fkr->for', weight_rows[time_tap, row_tap, column_tap], win...]
    ppermute x4, starting transfers between devices: 23.8 us -> 15 us  [extended(): lax.ppermute(lax.slice_in_dim(block, 0, width, axis=dim), axis, backward)]
    ppermute x4 -> x0, local copies, waits for them, and re-layouts: 6.3 us -> none  [the longest x2 3.15 us: extended(): lax.ppermute(lax.slice_in_dim(block, block.shape[dim] - width, None, axis...]
    ppermute x4, waiting for transfers between devices: 13.5 us -> 19.3 us  [extended(): lax.ppermute(lax.slice_in_dim(block, 0, width, axis=dim), axis, backward)]
    all_to_all x0 -> x1, waiting for transfers between devices: none -> 5.43 us  [convolve(): jax.lax.all_to_all(jnp.stack([source for _ in range(jax.lax.axis_size('ch...]
    ppermute x4, waiting for transfers between devices: 15.2 us -> 20.5 us  [extended(): lax.ppermute(lax.slice_in_dim(block, block.shape[dim] - width, None, axis...]
  transfers between devices with their start and end apart: 8 -> 9, of which waited for: 7 -> 8; matrix products, arithmetic and copies ran while one was open for 17% -> 6% of each run, Pallas kernels for 0% -> 0%
where the time goes in v1:
time: 176 us; the launch traced here: 175 us
  blocking collectives  57.4 us (33%)
  waiting for transfers between devices  45.3 us (26%)
  matrix products  31.7 us (18%)
  starting transfers between devices  31.3 us (18%)
  local copies, waits for them, and re-layouts  6.49 us (4%)
  other arithmetic  2.22 us (1%)
    all_to_all x3, blocking collectives, convolve(): jax.lax.all_to_all(jnp.stack([source for _ in range(jax.lax.axis_size('ch...  42.7 us
    dot_general x81, matrix products, causal_terms(): jnp.einsum('ok,fkr->for', weight_rows[time_tap, row_tap, column_tap], win...  26 us
    ppermute x4, waiting for transfers between devices, extended(): lax.ppermute(lax.slice_in_dim(block, block.shape[dim] - width, None, axis...  20.5 us
    ppermute x4, waiting for transfers between devices, extended(): lax.ppermute(lax.slice_in_dim(block, 0, width, axis=dim), axis, backward)  19.3 us
    ppermute x4, starting transfers between devices, extended(): lax.ppermute(lax.slice_in_dim(block, 0, width, axis=dim), axis, backward)  15 us
    psum x2, blocking collectives, activate(): total_sq = lax.psum(squares, 'chan')  14.7 us
    ppermute x4, starting transfers between devices, extended(): lax.ppermute(lax.slice_in_dim(block, block.shape[dim] - width, None, axis...  11.9 us
    dot_general x25, matrix products, upsample_terms(): jnp.einsum('ok,fkr->for', weight_rows[row_tap, column_tap], window, prefe...  5.74 us
  transfers between devices with their start and end apart: 9, of which 8 were waited for; matrix products, arithmetic and copies ran while one was open for 6% of the time, Pallas kernels for 0%

profile of v1, /device:TPU:128, one launch (start us, length us, event | category | flops | bytes accessed | tf_op | source)
XLA Modules:
  0.0 175.5 jit_solution(13320483096530738501)
XLA Ops:
  1.4 4.5 %all-to-all-start = ((bf16[4,4,4,225]{3,2,1,0:T(4,128)(2,1)}), bf16[4,4,4,225]{3,2,1,0:T(4,128)(2,1)S(1)}, u32[]{:S(2)}, u32[]{:S(2)}) async-start(bf16[4,4,4,225]{3,2,1,0:T(4,128)(2,1)} %stack.18), calls=%async_computation | async-start | bytes 65536 | tf_op jit(solution)/shard_map/all_to_all | solution.py:87
  5.9 5.4 %all-to-all-done = bf16[4,4,4,225]{3,2,1,0:T(4,128)(2,1)S(1)} async-done(((bf16[4,4,4,225]{3,2,1,0:T(4,128)(2,1)}), bf16[4,4,4,225]{3,2,1,0:T(4,128)(2,1)S(1)}, u32[]{:S(2)}, u32[]{:S(2)}) %all-to-all-start) | async-done | bytes 28832 | tf_op jit(solution)/shard_map/all_to_all | solution.py:87
  11.5 4.3 %collective-permute-start.1 = (bf16[4,16,161]{2,1,0:T(8,128)(2,1)S(1)}, bf16[4,16,161]{2,1,0:T(8,128)(2,1)S(1)}, u32[]{:S(2)}, u32[]{:S(2)}) collective-permute-start(bf16[4,16,161]{2,1,0:T(8,128)(2,1)S(1)} %get-tuple-element.27), channel_id=1, source_target_pairs={{4,0},{8,4},{12,8},{16,12},{20,16},{24,20},{28,24},{32,28},{36,32}... | collective-permute-start | bytes 61832 | tf_op jit(solution)/shard_map/ppermute | solution.py:20
  15.8 1.9 %collective-permute-start = (bf16[4,16,161]{2,1,0:T(8,128)(2,1)S(1)}, bf16[4,16,161]{2,1,0:T(8,128)(2,1)S(1)}, u32[]{:S(2)}, u32[]{:S(2)}) collective-permute-start(bf16[4,16,161]{2,1,0:T(8,128)(2,1)S(1)} %get-tuple-element.26), channel_id=1, source_target_pairs={{0,4},{4,8},{8,12},{12,16},{16,20},{20,24},{24,28},{28,32},{32,36}... | collective-permute-start | bytes 61832 | tf_op jit(solution)/shard_map/ppermute | solution.py:17
  23.6 2.2 %collective-permute-done = bf16[4,16,161]{2,1,0:T(8,128)(2,1)S(1)} collective-permute-done((bf16[4,16,161]{2,1,0:T(8,128)(2,1)S(1)}, bf16[4,16,161]{2,1,0:T(8,128)(2,1)S(1)}, u32[]{:S(2)}, u32[]{:S(2)}) %collective-permute-start) | collective-permute-done | bytes 20640 | tf_op jit(solution)/shard_map/ppermute | solution.py:17
  30.8 7.5 %psum.14 = f32[2,225]{1,0:T(2,128)S(1)} all-reduce(f32[2,225]{1,0:T(2,128)S(1)} %get-tuple-element.28), channel_id=1, replica_groups=mesh['tile'=64,'chan'=4] {'chan'}, use_global_device_ids=true, to_apply=%region_1.2 | all-reduce | flops 450 | bytes 3600 | tf_op jit(solution)/shard_map/psum | solution.py:102
  38.6 15.6 %all_to_all.20 = bf16[4,4,96,225]{3,2,1,0:T(8,128)(2,1)S(1)} all-to-all(bf16[4,4,96,225]{3,2,1,0:T(8,128)(2,1)S(1)} %stack.19), channel_id=1, replica_groups=mesh['tile'=64,'chan'=4] {'chan'}, dimensions={0} | all-to-all | bytes 1382400 | tf_op jit(solution)/shard_map/all_to_all | solution.py:87
  54.2 1.1 fusion.632
  55.8 6.7 %collective-permute-start.3 = (bf16[4,384,161]{1,2,0:T(8,128)(2,1)S(1)}, bf16[4,384,161]{1,2,0:T(8,128)(2,1)S(1)}, u32[]{:S(2)}, u32[]{:S(2)}) collective-permute-start(bf16[4,384,161]{1,2,0:T(8,128)(2,1)S(1)} %get-tuple-element.14), channel_id=1, source_target_pairs={{4,0},{8,4},{12,8},{16,12},{20,16},{24,20},{28,24},{32,28},{36,32}... | collective-permute-start | bytes 1483784 | tf_op jit(solution)/shard_map/ppermute | solution.py:20
  62.5 1.9 %collective-permute-start.2 = (bf16[4,384,161]{1,2,0:T(8,128)(2,1)S(1)}, bf16[4,384,161]{1,2,0:T(8,128)(2,1)S(1)}, u32[]{:S(2)}, u32[]{:S(2)}) collective-permute-start(bf16[4,384,161]{1,2,0:T(8,128)(2,1)S(1)} %get-tuple-element.13), channel_id=1, source_target_pairs={{0,4},{4,8},{8,12},{12,16},{16,20},{20,24},{24,28},{28,32},{32,36}... | collective-permute-start | bytes 1483784 | tf_op jit(solution)/shard_map/ppermute | solution.py:17
  65.2 7.9 %collective-permute-done.3 = bf16[4,384,161]{1,2,0:T(8,128)(2,1)S(1)} collective-permute-done((bf16[4,384,161]{1,2,0:T(8,128)(2,1)S(1)}, bf16[4,384,161]{1,2,0:T(8,128)(2,1)S(1)}, u32[]{:S(2)}, u32[]{:S(2)}) %collective-permute-start.3) | collective-permute-done | bytes 494624 | tf_op jit(solution)/shard_map/ppermute | solution.py:20
  74.3 7.2 %collective-permute-done.2 = bf16[4,384,161]{1,2,0:T(8,128)(2,1)S(1)} collective-permute-done((bf16[4,384,161]{1,2,0:T(8,128)(2,1)S(1)}, bf16[4,384,161]{1,2,0:T(8,128)(2,1)S(1)}, u32[]{:S(2)}, u32[]{:S(2)}) %collective-permute-start.2) | collective-permute-done | bytes 494624 | tf_op jit(solution)/shard_map/ppermute | solution.py:17
  87.5 7.2 %psum.15 = f32[2,225]{1,0:T(2,128)S(1)} all-reduce(f32[2,225]{1,0:T(2,128)S(1)} %get-tuple-element.30), channel_id=1, replica_groups=mesh['tile'=64,'chan'=4] {'chan'}, use_global_device_ids=true, to_apply=%region_3.4 | all-reduce | flops 450 | bytes 3600 | tf_op jit(solution)/shard_map/psum | solution.py:102
  95.0 15.7 %all_to_all.21 = bf16[4,4,96,225]{3,2,1,0:T(8,128)(2,1)S(1)} all-to-all(bf16[4,4,96,225]{3,2,1,0:T(8,128)(2,1)S(1)} %stack.20), channel_id=1, replica_groups=mesh['tile'=64,'chan'=4] {'chan'}, dimensions={0} | all-to-all | bytes 1382400 | tf_op jit(solution)/shard_map/all_to_all | solution.py:87
  110.7 1.1 fusion.631
  112.2 2.1 %collective-permute-start.5 = (bf16[4,384,161]{1,2,0:T(8,128)(2,1)S(1)}, bf16[4,384,161]{1,2,0:T(8,128)(2,1)S(1)}, u32[]{:S(2)}, u32[]{:S(2)}) collective-permute-start(bf16[4,384,161]{1,2,0:T(8,128)(2,1)S(1)} %get-tuple-element.12), channel_id=1, source_target_pairs={{4,0},{8,4},{12,8},{16,12},{20,16},{24,20},{28,24},{32,28},{36,32}... | collective-permute-start | bytes 1483784 | tf_op jit(solution)/shard_map/ppermute | solution.py:20
  114.3 4.1 %collective-permute-start.4 = (bf16[4,384,161]{1,2,0:T(8,128)(2,1)S(1)}, bf16[4,384,161]{1,2,0:T(8,128)(2,1)S(1)}, u32[]{:S(2)}, u32[]{:S(2)}) collective-permute-start(bf16[4,384,161]{1,2,0:T(8,128)(2,1)S(1)} %get-tuple-element.11), channel_id=1, source_target_pairs={{0,4},{4,8},{8,12},{12,16},{16,20},{20,24},{24,28},{28,32},{32,36}... | collective-permute-start | bytes 1483784 | tf_op jit(solution)/shard_map/ppermute | solution.py:17
  119.2 8.2 %collective-permute-done.5 = bf16[4,384,161]{1,2,0:T(8,128)(2,1)S(1)} collective-permute-done((bf16[4,384,161]{1,2,0:T(8,128)(2,1)S(1)}, bf16[4,384,161]{1,2,0:T(8,128)(2,1)S(1)}, u32[]{:S(2)}, u32[]{:S(2)}) %collective-permute-start.5) | collective-permute-done | bytes 494624 | tf_op jit(solution)/shard_map/ppermute | solution.py:20
  128.6 5.0 %collective-permute-done.4 = bf16[4,384,161]{1,2,0:T(8,128)(2,1)S(1)} collective-permute-done((bf16[4,384,161]{1,2,0:T(8,128)(2,1)S(1)}, bf16[4,384,161]{1,2,0:T(8,128)(2,1)S(1)}, u32[]{:S(2)}, u32[]{:S(2)}) %collective-permute-start.4) | collective-permute-done | bytes 494624 | tf_op jit(solution)/shard_map/ppermute | solution.py:17
  139.9 11.5 %all_to_all.22 = bf16[4,2,96,225]{3,2,1,0:T(8,128)(2,1)S(1)} all-to-all(bf16[4,2,96,225]{3,2,1,0:T(8,128)(2,1)S(1)} %stack.21), channel_id=1, replica_groups=mesh['tile'=64,'chan'=4] {'chan'}, dimensions={0} | all-to-all | bytes 691200 | tf_op jit(solution)/shard_map/all_to_all | solution.py:87
  152.4 1.9 %collective-permute-start.7 = (bf16[2,384,161]{1,2,0:T(8,128)(2,1)S(1)}, bf16[2,384,161]{1,2,0:T(8,128)(2,1)S(1)}, u32[]{:S(2)}, u32[]{:S(2)}) collective-permute-start(bf16[2,384,161]{1,2,0:T(8,128)(2,1)S(1)} %get-tuple-element.22), channel_id=1, source_target_pairs={{4,0},{8,4},{12,8},{16,12},{20,16},{24,20},{28,24},{32,28},{36,32}... | collective-permute-start | bytes 741896 | tf_op jit(solution)/shard_map/ppermute | solution.py:20
  154.3 3.9 %collective-permute-start.6 = (bf16[2,384,161]{1,2,0:T(8,128)(2,1)S(1)}, bf16[2,384,161]{1,2,0:T(8,128)(2,1)S(1)}, u32[]{:S(2)}, u32[]{:S(2)}) collective-permute-start(bf16[2,384,161]{1,2,0:T(8,128)(2,1)S(1)} %get-tuple-element.21), channel_id=1, source_target_pairs={{0,4},{4,8},{8,12},{12,16},{16,20},{20,24},{24,28},{28,32},{32,36}... | collective-permute-start | bytes 741896 | tf_op jit(solution)/shard_map/ppermute | solution.py:17
  158.7 3.2 %collective-permute-done.7 = bf16[2,384,161]{1,2,0:T(8,128)(2,1)S(1)} collective-permute-done((bf16[2,384,161]{1,2,0:T(8,128)(2,1)S(1)}, bf16[2,384,161]{1,2,0:T(8,128)(2,1)S(1)}, u32[]{:S(2)}, u32[]{:S(2)}) %collective-permute-start.7) | collective-permute-done | bytes 247328 | tf_op jit(solution)/shard_map/ppermute | solution.py:20
  161.9 6.1 %collective-permute-done.6 = bf16[2,384,161]{1,2,0:T(8,128)(2,1)S(1)} collective-permute-done((bf16[2,384,161]{1,2,0:T(8,128)(2,1)S(1)}, bf16[2,384,161]{1,2,0:T(8,128)(2,1)S(1)}, u32[]{:S(2)}, u32[]{:S(2)}) %collective-permute-start.6) | collective-permute-done | bytes 247328 | tf_op jit(solution)/shard_map/ppermute | solution.py:17
  (189 shorter events, 38.3 us)
Async XLA Ops:
  0.0 23.3 %copy-start.11 = (bf16[3,3,3,96,16]{3,4,2,1,0:T(8,128)(2,1)S(1)}, bf16[3,3,3,96,16]{3,4,2,1,0:T(8,128)(2,1)}, u32[]{:S(2)}) copy-start(bf16[3,3,3,96,16]{3,4,2,1,0:T(8,128)(2,1)} %param.16) | copy-start | bytes 248836
  1.4 9.9 %all-to-all-start = ((bf16[4,4,4,225]{3,2,1,0:T(4,128)(2,1)}), bf16[4,4,4,225]{3,2,1,0:T(4,128)(2,1)S(1)}, u32[]{:S(2)}, u32[]{:S(2)}) async-start(bf16[4,4,4,225]{3,2,1,0:T(4,128)(2,1)} %stack.18), calls=%async_computation | async-start | bytes 65536 | tf_op jit(solution)/shard_map/all_to_all | solution.py:87
  11.5 9.1 %collective-permute-start.1 = (bf16[4,16,161]{2,1,0:T(8,128)(2,1)S(1)}, bf16[4,16,161]{2,1,0:T(8,128)(2,1)S(1)}, u32[]{:S(2)}, u32[]{:S(2)}) collective-permute-start(bf16[4,16,161]{2,1,0:T(8,128)(2,1)S(1)} %get-tuple-element.27), channel_id=1, source_target_pairs={{4,0},{8,4},{12,8},{16,12},{20,16},{24,20},{28,24},{32,28},{36,32}... | collective-permute-start | bytes 61832 | tf_op jit(solution)/shard_map/ppermute | solution.py:20
  15.8 10.0 %collective-permute-start = (bf16[4,16,161]{2,1,0:T(8,128)(2,1)S(1)}, bf16[4,16,161]{2,1,0:T(8,128)(2,1)S(1)}, u32[]{:S(2)}, u32[]{:S(2)}) collective-permute-start(bf16[4,16,161]{2,1,0:T(8,128)(2,1)S(1)} %get-tuple-element.26), channel_id=1, source_target_pairs={{0,4},{4,8},{8,12},{12,16},{16,20},{20,24},{24,28},{28,32},{32,36}... | collective-permute-start | bytes 61832 | tf_op jit(solution)/shard_map/ppermute | solution.py:17
  29.9 8.4 %copy-start.15 = (f32[96]{0:T(128)S(1)}, f32[96]{0:T(128)}, u32[]{:S(2)}) copy-start(f32[96]{0:T(128)} %param.19) | copy-start | bytes 1156
  29.9 8.6 %copy-start.12 = (bf16[2,96,225]{2,1,0:T(8,128)(2,1)S(1)}, bf16[2,96,225]{2,1,0:T(8,128)(2,1)}, u32[]{:S(2)}) copy-start(bf16[2,96,225]{2,1,0:T(8,128)(2,1)} %param.18) | copy-start | bytes 259204
  30.8 23.4 %copy-start.3 = (f32[2,225,96]{1,2,0:T(8,128)}, f32[2,225,96]{1,2,0:T(8,128)S(1)}, u32[]{:S(2)}) copy-start(f32[2,225,96]{1,2,0:T(8,128)S(1)} %get-tuple-element.29) | copy-start | bytes 518404
  55.3 9.2 %copy-start.1 = (bf16[3,3,3,96,384]{4,3,2,1,0:T(8,128)(2,1)S(1)}, bf16[3,3,3,96,384]{4,3,2,1,0:T(8,128)(2,1)}, u32[]{:S(2)}) copy-start(bf16[3,3,3,96,384]{4,3,2,1,0:T(8,128)(2,1)} %param.20) | copy-start | bytes 5971972
  55.7 8.8 %copy-start.9 = (bf16[2,4,96,225]{3,2,0,1:T(8,128)(2,1)S(1)}, bf16[2,4,96,225]{3,2,0,1:T(8,128)(2,1)}, u32[]{:S(2)}) copy-start(bf16[2,4,96,225]{3,2,0,1:T(8,128)(2,1)} %get-tuple-element.9) | copy-start | bytes 1036804
  55.7 9.0 %copy-start.7 = (bf16[2,4,96,225]{3,2,0,1:T(8,128)(2,1)S(1)}, bf16[2,4,96,225]{3,2,0,1:T(8,128)(2,1)}, u32[]{:S(2)}) copy-start(bf16[2,4,96,225]{3,2,0,1:T(8,128)(2,1)} %get-tuple-element.10) | copy-start | bytes 1036804
  55.7 9.1 %copy-start.5 = (bf16[2,4,96,225]{3,2,0,1:T(8,128)(2,1)S(1)}, bf16[2,4,96,225]{3,2,0,1:T(8,128)(2,1)}, u32[]{:S(2)}) copy-start(bf16[2,4,96,225]{3,2,0,1:T(8,128)(2,1)} %get-tuple-element.8) | copy-start | bytes 1036804
  55.8 17.3 %collective-permute-start.3 = (bf16[4,384,161]{1,2,0:T(8,128)(2,1)S(1)}, bf16[4,384,161]{1,2,0:T(8,128)(2,1)S(1)}, u32[]{:S(2)}, u32[]{:S(2)}) collective-permute-start(bf16[4,384,161]{1,2,0:T(8,128)(2,1)S(1)} %get-tuple-element.14), channel_id=1, source_target_pairs={{4,0},{8,4},{12,8},{16,12},{20,16},{24,20},{28,24},{32,28},{36,32}... | collective-permute-start | bytes 1483784 | tf_op jit(solution)/shard_map/ppermute | solution.py:20
  62.5 19.0 %collective-permute-start.2 = (bf16[4,384,161]{1,2,0:T(8,128)(2,1)S(1)}, bf16[4,384,161]{1,2,0:T(8,128)(2,1)S(1)}, u32[]{:S(2)}, u32[]{:S(2)}) collective-permute-start(bf16[4,384,161]{1,2,0:T(8,128)(2,1)S(1)} %get-tuple-element.13), channel_id=1, source_target_pairs={{0,4},{4,8},{8,12},{12,16},{16,20},{20,24},{24,28},{28,32},{32,36}... | collective-permute-start | bytes 1483784 | tf_op jit(solution)/shard_map/ppermute | solution.py:17
  87.1 7.6 %copy-start.16 = (f32[96]{0:T(128)S(1)}, f32[96]{0:T(128)}, u32[]{:S(2)}) copy-start(f32[96]{0:T(128)} %param.23) | copy-start | bytes 1156
  87.1 7.7 %copy-start.13 = (bf16[2,96,225]{2,1,0:T(8,128)(2,1)S(1)}, bf16[2,96,225]{2,1,0:T(8,128)(2,1)}, u32[]{:S(2)}) copy-start(bf16[2,96,225]{2,1,0:T(8,128)(2,1)} %param.22) | copy-start | bytes 259204
  111.8 6.7 %copy-start.2 = (bf16[3,3,3,96,384]{4,3,2,1,0:T(8,128)(2,1)S(1)}, bf16[3,3,3,96,384]{4,3,2,1,0:T(8,128)(2,1)}, u32[]{:S(2)}) copy-start(bf16[3,3,3,96,384]{4,3,2,1,0:T(8,128)(2,1)} %param.24) | copy-start | bytes 5971972
  112.1 6.3 %copy-start.10 = (bf16[2,4,96,225]{3,2,0,1:T(8,128)(2,1)S(1)}, bf16[2,4,96,225]{3,2,0,1:T(8,128)(2,1)}, u32[]{:S(2)}) copy-start(bf16[2,4,96,225]{3,2,0,1:T(8,128)(2,1)} %get-tuple-element.6) | copy-start | bytes 1036804
  112.1 6.6 %copy-start.8 = (bf16[2,4,96,225]{3,2,0,1:T(8,128)(2,1)S(1)}, bf16[2,4,96,225]{3,2,0,1:T(8,128)(2,1)}, u32[]{:S(2)}) copy-start(bf16[2,4,96,225]{3,2,0,1:T(8,128)(2,1)} %get-tuple-element.7) | copy-start | bytes 1036804
  112.1 6.6 %copy-start.6 = (bf16[2,4,96,225]{3,2,0,1:T(8,128)(2,1)S(1)}, bf16[2,4,96,225]{3,2,0,1:T(8,128)(2,1)}, u32[]{:S(2)}) copy-start(bf16[2,4,96,225]{3,2,0,1:T(8,128)(2,1)} %get-tuple-element.5) | copy-start | bytes 1036804
  112.2 15.1 %collective-permute-start.5 = (bf16[4,384,161]{1,2,0:T(8,128)(2,1)S(1)}, bf16[4,384,161]{1,2,0:T(8,128)(2,1)S(1)}, u32[]{:S(2)}, u32[]{:S(2)}) collective-permute-start(bf16[4,384,161]{1,2,0:T(8,128)(2,1)S(1)} %get-tuple-element.12), channel_id=1, source_target_pairs={{4,0},{8,4},{12,8},{16,12},{20,16},{24,20},{28,24},{32,28},{36,32}... | collective-permute-start | bytes 1483784 | tf_op jit(solution)/shard_map/ppermute | solution.py:20
  114.3 19.2 %collective-permute-start.4 = (bf16[4,384,161]{1,2,0:T(8,128)(2,1)S(1)}, bf16[4,384,161]{1,2,0:T(8,128)(2,1)S(1)}, u32[]{:S(2)}, u32[]{:S(2)}) collective-permute-start(bf16[4,384,161]{1,2,0:T(8,128)(2,1)S(1)} %get-tuple-element.11), channel_id=1, source_target_pairs={{0,4},{4,8},{8,12},{12,16},{16,20},{20,24},{24,28},{28,32},{32,36}... | collective-permute-start | bytes 1483784 | tf_op jit(solution)/shard_map/ppermute | solution.py:17
  139.8 11.8 %copy-start = (bf16[3,3,48,384]{3,2,1,0:T(8,128)(2,1)S(1)}, bf16[3,3,48,384]{3,2,1,0:T(8,128)(2,1)}, u32[]{:S(2)}) copy-start(bf16[3,3,48,384]{3,2,1,0:T(8,128)(2,1)} %param.26) | copy-start | bytes 995332
  152.4 9.5 %collective-permute-start.7 = (bf16[2,384,161]{1,2,0:T(8,128)(2,1)S(1)}, bf16[2,384,161]{1,2,0:T(8,128)(2,1)S(1)}, u32[]{:S(2)}, u32[]{:S(2)}) collective-permute-start(bf16[2,384,161]{1,2,0:T(8,128)(2,1)S(1)} %get-tuple-element.22), channel_id=1, source_target_pairs={{4,0},{8,4},{12,8},{16,12},{20,16},{24,20},{28,24},{32,28},{36,32}... | collective-permute-start | bytes 741896 | tf_op jit(solution)/shard_map/ppermute | solution.py:20
  154.3 13.7 %collective-permute-start.6 = (bf16[2,384,161]{1,2,0:T(8,128)(2,1)S(1)}, bf16[2,384,161]{1,2,0:T(8,128)(2,1)S(1)}, u32[]{:S(2)}, u32[]{:S(2)}) collective-permute-start(bf16[2,384,161]{1,2,0:T(8,128)(2,1)S(1)} %get-tuple-element.21), channel_id=1, source_target_pairs={{0,4},{4,8},{8,12},{12,16},{16,20},{20,24},{24,28},{28,32},{32,36}... | collective-permute-start | bytes 741896 | tf_op jit(solution)/shard_map/ppermute | solution.py:17
  (5 other events, 5.0 us)
